TPU v7x, 32 devices: a whole 2x2x4 slice. The times are simulated.
32 devices in a mesh: grp: 2 (over y), req: 4 (over x, core), fsdp: 4 (over z).
Axes of the slice: x: 2, y: 2, z: 4, core: 2. Of those that a mesh axis runs over, the one named last changes fastest.
Arguments:
- hy_q: bfloat16 [8, 1024, 4096], P(('grp', 'req'), None, 'fsdp'), parts along dimension 0, may hold values from -6 to 6
- hy_k: bfloat16 [8, 1024, 4096], P(('grp', 'req'), None, 'fsdp'), parts along dimension 0, may hold values from -6 to 6
- hy_v: bfloat16 [8, 1024, 4096], P(('grp', 'req'), None, 'fsdp'), parts along dimension 0, may hold values from -6 to 6
- filter_taps: bfloat16 [4096, 128], P('fsdp', 'req'), may hold values from -0.8984375 to 0.8984375
- filter_decay: float32 [4096], P('fsdp'), may hold values from 0.003 to 0.08
- hy_cache: bfloat16 [32, 128, 4096], P(('grp', 'req'), None, 'fsdp'), parts along dimension 0, may hold values from -6 to 6
- at_q: bfloat16 [8, 1024, 4096], P(('grp', 'req'), None, 'fsdp'), parts along dimension 0, may hold values from -12 to 12, as said below
- at_k: bfloat16 [8, 1024, 4096], P(('grp', 'req'), None, 'fsdp'), parts along dimension 0, may hold values from -6 to 6
- at_v: bfloat16 [8, 1024, 4096], P(('grp', 'req'), None, 'fsdp'), parts along dimension 0, may hold values from -6 to 6
- kv_cache: bfloat16 [32, 2, 128, 4096], P(('grp', 'req'), None, None, 'fsdp'), parts along dimension 0, may hold values from -6 to 6, as said below
- prefix_owner: int32 [8, 8], P('grp'), parts along dimension 0, may hold values from 0 to 3, as said below
- prefix_slot: int32 [8, 8], P('grp'), parts along dimension 0, may hold values from 0 to 3, as said below
- prefix_count: int32 [8], P('grp'), parts along dimension 0, may hold values from 1 to 8, as said below
- new_length: int32 [8], P(('grp', 'req')), parts along dimension 0, may hold values from 1 to 1024, as said below
Outputs:
- hy_out: bfloat16 [8, 1024, 4096], P(('grp', 'req'), None, 'fsdp'), parts along dimension 0
- at_out: bfloat16 [8, 1024, 4096], P(('grp', 'req'), None, 'fsdp'), parts along dimension 0
There are 2 independent parts, one for each index of `grp`. A program takes and returns all parts, laid end to end along the dimension named above; an argument that names none is the same for every part. Nothing has to cross between parts.
Inputs may be any that keep to these rules, and one draw needn't show every extreme that they name: `prefix_owner`: the first prefix_count[r] entries of row r, read with prefix_slot, name distinct cache blocks, at most 2 of them with one owner; in every draw some request has exactly 2 entries at every owner. Entries past the count are not read. `prefix_slot`: read with prefix_owner. `prefix_count`: some request has 8. `new_length`: some request has 1024. `at_q`: Real-valued entries. `kv_cache`: Real-valued entries.
All inputs are finite; a program needn't handle non-finite values.
Results may differ from a plain program's by a relative error of at most 0.0057.
Values may be sent and summed in bfloat16 or wider, within the bound.
No kernel may reach another device: no remote copies, remote signals or barrier semaphores. Data moves between devices by JAX's collectives and lax.ppermute only.
A program may use at most 128 MiB of HBM per device.

v0:
```python
import math
import jax
import jax.numpy as jnp
from jax import lax
from jax.sharding import PartitionSpec as P

HD = 128
CAP = 2


def causal_filter(extended, kernel):
    taps_first = jnp.flip(kernel, axis=1).T[:, None, :]
    return lax.conv_general_dilated(
        extended,
        taps_first,
        (1,),
        "VALID",
        dimension_numbers=("NWC", "WIO", "NWC"),
        feature_group_count=kernel.shape[0],
        preferred_element_type=jnp.float32,
    )


def fold_keys(state_carry, queries, key_rows, value_rows, visible):
    running_max, running_sum, weighted = state_carry
    scores = jnp.einsum("qhd,khd->hqk", queries, key_rows, preferred_element_type=jnp.float32) * (
        1.0 / math.sqrt(queries.shape[2])
    )
    scores = jnp.where(visible[None], scores, -1e30)
    new_max = jnp.maximum(running_max, jnp.max(scores, axis=2))
    weight = jnp.where(visible[None], jnp.exp(scores - new_max[:, :, None]), 0.0)
    shrink = jnp.exp(running_max - new_max)
    running_sum = running_sum * shrink + jnp.sum(weight, axis=2)
    weighted = weighted * shrink[:, :, None] + jnp.einsum(
        "hqk,khd->hqd", weight.astype(jnp.bfloat16), value_rows, preferred_element_type=jnp.float32
    )
    return (new_max, running_sum, weighted)


def fetch_state(outgoing):
    return lax.all_to_all(outgoing, "req", split_axis=0, concat_axis=0, tiled=True)


def per_device(
    hy_q,
    hy_k,
    hy_v,
    filter_taps,
    filter_decay,
    hy_cache,
    at_q,
    at_k,
    at_v,
    kv_cache,
    prefix_owner,
    prefix_slot,
    prefix_count,
    new_length,
):
    device_index = lax.axis_index("req")
    new_rows = hy_q.shape[1]
    requests = prefix_owner.shape[0]
    entries = prefix_owner.shape[1]
    block_rows = hy_cache.shape[1]
    positions = jnp.arange(new_rows, dtype=jnp.int32)
    row_live = positions < new_length[0]
    filter_full = lax.all_gather(filter_taps, "req", axis=1, tiled=True)
    filter_len = filter_full.shape[1]
    lag_steps = jnp.arange(filter_len, dtype=jnp.float32)
    kernel = (
        filter_full.astype(jnp.float32) * jnp.exp(-filter_decay[:, None] * lag_steps[None, :])
    ).astype(jnp.bfloat16)
    last_entry = (prefix_count - 1)[:, None]
    last_owner = jnp.take_along_axis(prefix_owner, last_entry, axis=1)[:, 0]
    last_slot = jnp.take_along_axis(prefix_slot, last_entry, axis=1)[:, 0]
    outgoing = hy_cache[last_slot]
    my_last_owner = lax.dynamic_index_in_dim(last_owner, device_index, 0, keepdims=False)
    heads_dev = at_q.shape[2] // HD
    queries = at_q[0].reshape(new_rows, heads_dev, HD)
    carried = (
        jnp.full((heads_dev, new_rows), -1e30, jnp.float32),
        jnp.zeros((heads_dev, new_rows), jnp.float32),
        jnp.zeros((heads_dev, new_rows, HD), jnp.float32),
    )
    key_block = math.gcd(new_rows, 512)
    block_count = new_rows // key_block
    fresh_keys = at_k[0].reshape(block_count, key_block, heads_dev, HD)
    fresh_values = at_v[0].reshape(block_count, key_block, heads_dev, HD)
    block_starts = jnp.arange(block_count, dtype=jnp.int32) * key_block

    def fresh_step(state_carry, operands):
        key_rows, value_rows, start_row = operands
        visible = (start_row + jnp.arange(key_block, dtype=jnp.int32))[None, :] <= positions[
            :, None
        ]
        return (fold_keys(state_carry, queries, key_rows, value_rows, visible), None)

    carried, unused = lax.scan(fresh_step, carried, (fresh_keys, fresh_values, block_starts))
    my_owners = lax.dynamic_index_in_dim(prefix_owner, device_index, 0, keepdims=False)
    my_count = lax.dynamic_index_in_dim(prefix_count, device_index, 0, keepdims=False)
    entry_live = jnp.arange(entries, dtype=jnp.int32) < my_count
    all_live = jnp.arange(entries, dtype=jnp.int32)[None, :] < prefix_count[:, None]
    entry_mine = jnp.logical_and(all_live, prefix_owner == device_index)
    mine_count = entry_mine.astype(jnp.int32)
    entry_rank = jnp.cumsum(mine_count, axis=1) - mine_count
    slot_numbers = jnp.arange(CAP, dtype=jnp.int32)
    choose = jnp.logical_and(
        entry_mine[:, :, None], entry_rank[:, :, None] == slot_numbers[None, None, :]
    )
    local_slot = jnp.sum(jnp.where(choose, prefix_slot[:, :, None], 0), axis=1)
    outgoing_blocks = kv_cache[local_slot]
    incoming = fetch_state(outgoing)
    incoming_blocks = lax.all_to_all(
        outgoing_blocks, "req", split_axis=0, concat_axis=0, tiled=True
    )
    owner_ids = jnp.arange(requests, dtype=jnp.int32)
    per_owner = jnp.sum(
        jnp.logical_and(entry_live[:, None], my_owners[:, None] == owner_ids[None, :]).astype(
            jnp.int32
        ),
        axis=0,
    )
    slot_used = slot_numbers[None, :] < per_owner[:, None]

    def owner_step(state_carry, operands):
        block_pair, flags = operands
        key_rows = block_pair[:, 0].reshape(-1, heads_dev, HD)
        value_rows = block_pair[:, 1].reshape(-1, heads_dev, HD)
        visible = jnp.repeat(flags, block_rows)[None, :]
        return (fold_keys(state_carry, queries, key_rows, value_rows, visible), None)

    carried, unused = lax.scan(owner_step, carried, (incoming_blocks, slot_used))
    prior_state = lax.dynamic_index_in_dim(incoming, my_last_owner, 0, keepdims=True)
    gated = (hy_k.astype(jnp.float32) * hy_v.astype(jnp.float32)).astype(jnp.bfloat16)
    extended = jnp.concatenate([prior_state, gated], axis=1)
    offset = block_rows - filter_len + 1
    mixed_sum = causal_filter(extended, kernel)[:, offset : offset + new_rows]
    hy_out = jnp.where(row_live[None, :, None], hy_q.astype(jnp.float32) * mixed_sum, 0.0).astype(
        jnp.bfloat16
    )
    running_max, running_sum, weighted = carried
    attended = weighted / running_sum[:, :, None]
    attended = jnp.transpose(attended, (1, 0, 2)).reshape(new_rows, heads_dev * HD)
    at_out = jnp.where(row_live[:, None], attended, 0.0).astype(jnp.bfloat16)[None]
    return (hy_out, at_out)


def solution(mesh):
    placed = (
        P(("grp", "req"), None, "fsdp"),
        P(("grp", "req"), None, "fsdp"),
        P(("grp", "req"), None, "fsdp"),
        P("fsdp", "req"),
        P("fsdp"),
        P(("grp", "req"), None, "fsdp"),
        P(("grp", "req"), None, "fsdp"),
        P(("grp", "req"), None, "fsdp"),
        P(("grp", "req"), None, "fsdp"),
        P(("grp", "req"), None, None, "fsdp"),
        P("grp", None),
        P("grp", None),
        P("grp"),
        P(("grp", "req")),
    )
    return jax.shard_map(
        per_device,
        mesh=mesh,
        in_specs=placed,
        out_specs=(P(("grp", "req"), None, "fsdp"), P(("grp", "req"), None, "fsdp")),
        check_vma=False,
    )
```

profile of v0, /device:TPU:19, one launch (start us, length us, event | category | flops | bytes accessed | tf_op | source)
XLA Modules:
  0.0 356.1 jit_solution(8966804692607989775)
XLA Ops:
  1.5 1.3 gather_fusion.3
  2.9 1.3 gather_fusion.2
  4.9 2.9 gather_fusion
  7.7 5.1 %all-to-all-start = ((bf16[4,128,1024]{2,1,0:T(8,128)(2,1)}), bf16[4,128,1024]{2,1,0:T(8,128)(2,1)}, u32[]{:S(2)}, u32[]{:S(2)}) async-start(bf16[4,128,1024]{2,1,0:T(8,128)(2,1)} %gather_fusion), calls=%async_computation | async-start | bytes 2097152 | tf_op jit(solution)/shard_map/all_to_all | solution.py:41
  15.4 12.6 %all_gather.3 = bf16[1024,128]{0,1:T(8,128)(2,1)S(1)} all-gather(bf16[1024,32]{0,1:T(8,128)(2,1)S(1)} %copy-done.12), channel_id=1, replica_groups=mesh['grp'=2,'req'=4,'fsdp'=4] {'req'}, dimensions={1}, use_global_device_ids=true | all-gather | bytes 327680 | tf_op jit(solution)/shard_map/all_gather | solution.py:67
  29.6 3.5 copy.75
  33.2 3.9 %copy.60 = bf16[1,1024,1024]{1,2,0:T(8,128)(2,1)} copy(bf16[1,1024,1024]{2,1,0:T(8,128)(2,1)} %param.26) | data formatting | bytes 4194304 | tf_op args[6]
  37.1 3.9 %copy.62 = bf16[1024,8,128]{2,0,1:T(8,128)(2,1)} copy(bf16[1024,8,128]{0,2,1:T(8,128)(2,1)} %bitcast.162) | data formatting | bytes 4194304
  41.0 3.5 copy.76
  44.6 64.6 %while.30 = (s32[]{:T(128)}, f32[8,1024]{1,0:T(8,128)S(1)}, f32[8,1024]{1,0:T(8,128)S(1)}, f32[8,1024,128]{2,1,0:T(8,128)}, s32[2]{0:T(128)S(1)}, /*index=5*/bf1...) while((s32[]{:T(128)}, f32[8,1024]{1,0:T(8,128)S(1)}, ...), condition=%wide.region_3.5_spmd.clone, body=%wide.region_0.4_spmd.clone.sunk | while | flops 2205721088 | bytes 115872000 | solution.py:98
  46.3 2.8 constant_dynamic-slice_fusion.10
  49.0 7.5 %fusion.90 = (f32[8,1024]{1,0:T(8,128)S(1)}, f32[8,512,1024]{2,1,0:T(8,128)}) fusion(pred[1024,512]{0,1:T(8,128)(4,1)S(1)} %iota_compare_fusion.9, bf16[1024,8,128]{2,0,1:T(8,128)(2,1)S(1)} %copy-done.2, bf16[1,512,8,128]{3,2,1,0:T(8,128)(2,1)S(1)} %get-tuple-element.325), kind=kOutput, calls=%fused_computation.34.clone.1 | convolution fusion | flops 1086316544 | bytes 20480000 | tf_op jit(solution)/shard_map/while/body/eval_jaxpr/qhd,khd->hqk/dot_general | solution.py:26
  56.5 8.6 %fusion.91 = f32[8,1024]{1,0:T(8,128)S(1)} fusion(f32[8,512,1024]{2,1,0:T(8,128)} %get-tuple-element.327, f32[8,1024]{1,0:T(8,128)S(1)} %select_maximum_fusion.2, pred[1024,512]{0,1:T(8,128)(4,1)S(1)} %iota_compare_fusion.9), kind=kLoop, calls=%fused_computation.36.clone.1 | loop fusion | flops 20963328 | bytes 17367040 | tf_op jit(solution)/shard_map/while/body/eval_jaxpr/reduce_sum | solution.py:33
  65.2 9.7 %fusion.93 = f32[8,1024,128]{2,1,0:T(8,128)S(1)} fusion(f32[8,1024,128]{2,1,0:T(8,128)S(1)} %copy-done.7, f32[8,1024]{1,0:T(8,128)S(1)} %get-tuple-element.329, pred[]{:T(512)S(6)} %compare.29, f32[8,512,1024]{2,1,0:T(8,128)} %get-tuple-element.327, f32[8,1024]{1,0:T(8,128)S(1)} %select_maximum_fusion.2, ...), kind=kOutput, calls=%fused_computation.40.clone.1 | convolution fusion | flops 1097859072 | bytes 26804224 | tf_op jit(solution)/shard_map/while/body/eval_jaxpr/hqk,khd->hqd/dot_general | solution.py:34
  74.9 1.9 copy-done.8
  78.6 2.8 constant_dynamic-slice_fusion.10
  81.3 7.5 %fusion.90 = (f32[8,1024]{1,0:T(8,128)S(1)}, f32[8,512,1024]{2,1,0:T(8,128)}) fusion(pred[1024,512]{0,1:T(8,128)(4,1)S(1)} %iota_compare_fusion.9, bf16[1024,8,128]{2,0,1:T(8,128)(2,1)S(1)} %copy-done.2, bf16[1,512,8,128]{3,2,1,0:T(8,128)(2,1)S(1)} %get-tuple-element.325), kind=kOutput, calls=%fused_computation.34.clone.1 | convolution fusion | flops 1086316544 | bytes 20480000 | tf_op jit(solution)/shard_map/while/body/eval_jaxpr/qhd,khd->hqk/dot_general | solution.py:26
  88.8 8.6 %fusion.91 = f32[8,1024]{1,0:T(8,128)S(1)} fusion(f32[8,512,1024]{2,1,0:T(8,128)} %get-tuple-element.327, f32[8,1024]{1,0:T(8,128)S(1)} %select_maximum_fusion.2, pred[1024,512]{0,1:T(8,128)(4,1)S(1)} %iota_compare_fusion.9), kind=kLoop, calls=%fused_computation.36.clone.1 | loop fusion | flops 20963328 | bytes 17367040 | tf_op jit(solution)/shard_map/while/body/eval_jaxpr/reduce_sum | solution.py:33
  97.4 9.7 %fusion.93 = f32[8,1024,128]{2,1,0:T(8,128)S(1)} fusion(f32[8,1024,128]{2,1,0:T(8,128)S(1)} %copy-done.7, f32[8,1024]{1,0:T(8,128)S(1)} %get-tuple-element.329, pred[]{:T(512)S(6)} %compare.29, f32[8,512,1024]{2,1,0:T(8,128)} %get-tuple-element.327, f32[8,1024]{1,0:T(8,128)S(1)} %select_maximum_fusion.2, ...), kind=kOutput, calls=%fused_computation.40.clone.1 | convolution fusion | flops 1097859072 | bytes 26804224 | tf_op jit(solution)/shard_map/while/body/eval_jaxpr/hqk,khd->hqd/dot_general | solution.py:34
  107.2 1.9 copy-done.8
  110.3 2.8 gather_fusion.1
  113.9 3.2 multiply_convert_fusion
  117.1 6.3 %all-to-all-start.1 = ((bf16[4,2,2,128,1024]{4,3,2,1,0:T(8,128)(2,1)}), bf16[4,2,2,128,1024]{4,3,2,1,0:T(8,128)(2,1)}, u32[]{:S(2)}, u32[]{:S(2)}) async-start(bf16[4,2,2,128,1024]{4,3,2,1,0:T(8,128)(2,1)} %bitcast.159), calls=%async_computation.1 | async-start | bytes 8388608 | tf_op jit(solution)/shard_map/all_to_all | solution.py:113
  125.1 1.3 copy.57
  127.7 159.2 %broadcast_select_fusion = f32[8,144,1024]{2,0,1:T(8,128)S(1)} fusion(pred[8,144]{0,1:T(8,128)(4,1)S(1)} %copy-done.16, bf16[128,1,1024]{2,0,1:T(8,128)(2,1)S(1)} %bitcast.165, bf16[8,271,1024]{2,0,1:T(8,128)(2,1)S(1)} %fusion.70), kind=kOutput, calls=%fused_computation.73 | convolution fusion | flops 303169536 | bytes 9421952 | tf_op jit(solution)/shard_map/slice | solution.py:137
  286.9 2.7 copy.59
  289.7 1.8 fusion.47
  291.6 51.5 %while.29 = (s32[]{:T(128)}, f32[8,1024]{1,0:T(8,128)S(1)}, f32[8,1024]{1,0:T(8,128)S(1)}, f32[8,1024,128]{2,1,0:T(8,128)}, pred[4,2]{1,0:T(4,128)(4,1)S(1)}, /*...) while((s32[]{:T(128)}, f32[8,1024]{1,0:T(8,128)S(1)}, ...), condition=%wide.region_10.12_spmd, body=%wide.region_7.11_spmd.sunk | while | flops 1103118336 | bytes 77071520 | solution.py:132
  293.1 1.4 bitcast_reduce_fusion.2
  294.5 2.3 fusion.87
  297.0 5.5 %multiply_add_fusion.5 = f32[8,1024,128]{2,1,0:T(8,128)S(1)} fusion(f32[8,1024,128]{2,1,0:T(8,128)S(1)} %copy-done.9, f32[8,1024]{1,0:T(8,128)S(1)} %get-tuple-element.315, f32[8,256,1024]{2,1,0:T(8,128)S(1)} %get-tuple-element.313, f32[8,1024]{1,0:T(8,128)S(1)} %max.10, pred[256]{0:T(512)(128)(4,1)S(1)} %broadcast_bitcast_fusion.2, ...), kind=kOutput, calls=%fused_computation.13.clone.1 | convolution fusion | flops 549453824 | bytes 17367296 | tf_op jit(solution)/shard_map/while/body/eval_jaxpr/hqk,khd->hqd/dot_general | solution.py:34
  302.5 1.9 copy-done.10
  306.0 1.4 bitcast_reduce_fusion.2
  307.4 2.3 fusion.87
  309.9 5.5 %multiply_add_fusion.5 = f32[8,1024,128]{2,1,0:T(8,128)S(1)} fusion(f32[8,1024,128]{2,1,0:T(8,128)S(1)} %copy-done.9, f32[8,1024]{1,0:T(8,128)S(1)} %get-tuple-element.315, f32[8,256,1024]{2,1,0:T(8,128)S(1)} %get-tuple-element.313, f32[8,1024]{1,0:T(8,128)S(1)} %max.10, pred[256]{0:T(512)(128)(4,1)S(1)} %broadcast_bitcast_fusion.2, ...), kind=kOutput, calls=%fused_computation.13.clone.1 | convolution fusion | flops 549453824 | bytes 17367296 | tf_op jit(solution)/shard_map/while/body/eval_jaxpr/hqk,khd->hqd/dot_general | solution.py:34
  315.4 1.9 copy-done.10
  318.8 1.4 bitcast_reduce_fusion.2
  320.3 2.3 fusion.87
  322.7 5.5 %multiply_add_fusion.5 = f32[8,1024,128]{2,1,0:T(8,128)S(1)} fusion(f32[8,1024,128]{2,1,0:T(8,128)S(1)} %copy-done.9, f32[8,1024]{1,0:T(8,128)S(1)} %get-tuple-element.315, f32[8,256,1024]{2,1,0:T(8,128)S(1)} %get-tuple-element.313, f32[8,1024]{1,0:T(8,128)S(1)} %max.10, pred[256]{0:T(512)(128)(4,1)S(1)} %broadcast_bitcast_fusion.2, ...), kind=kOutput, calls=%fused_computation.13.clone.1 | convolution fusion | flops 549453824 | bytes 17367296 | tf_op jit(solution)/shard_map/while/body/eval_jaxpr/hqk,khd->hqd/dot_general | solution.py:34
  328.2 1.9 copy-done.10
  331.7 1.4 bitcast_reduce_fusion.2
  333.1 2.3 fusion.87
  335.6 5.5 %multiply_add_fusion.5 = f32[8,1024,128]{2,1,0:T(8,128)S(1)} fusion(f32[8,1024,128]{2,1,0:T(8,128)S(1)} %copy-done.9, f32[8,1024]{1,0:T(8,128)S(1)} %get-tuple-element.315, f32[8,256,1024]{2,1,0:T(8,128)S(1)} %get-tuple-element.313, f32[8,1024]{1,0:T(8,128)S(1)} %max.10, pred[256]{0:T(512)(128)(4,1)S(1)} %broadcast_bitcast_fusion.2, ...), kind=kOutput, calls=%fused_computation.13.clone.1 | convolution fusion | flops 549453824 | bytes 17367296 | tf_op jit(solution)/shard_map/while/body/eval_jaxpr/hqk,khd->hqd/dot_general | solution.py:34
  341.1 1.9 copy-done.10
  343.0 2.9 divide_bitcast_fusion
  345.9 2.7 copy.67
  348.6 4.2 %reshape.131 = bf16[1,1024,1024]{2,1,0:T(8,128)(2,1)} reshape(bf16[1024,8,128]{2,1,0:T(8,128)(2,1)} %copy.67) | data formatting | bytes 4194304 | tf_op jit(solution)/shard_map/reshape | solution.py:143
  352.7 3.3 select_convert_fusion
  (130 shorter events, 18.3 us)
Async XLA Ops:
  0.6 109.7 %copy-start = (bf16[4,2,128,1024]{3,2,1,0:T(8,128)(2,1)S(1)}, bf16[4,2,128,1024]{3,2,1,0:T(8,128)(2,1)}, u32[]{:S(2)}) copy-start(bf16[4,2,128,1024]{3,2,1,0:T(8,128)(2,1)} %param.29) | copy-start | bytes 6291460
  0.6 14.1 %copy-start.15 = (s32[4]{0:T(128)S(1)}, s32[4]{0:T(128)}, u32[]{:S(2)}) copy-start(s32[4]{0:T(128)} %param.32) | copy-start | bytes 52
  0.7 14.0 %copy-start.4 = (s32[4,8]{1,0:T(4,128)S(1)}, s32[4,8]{1,0:T(4,128)}, u32[]{:S(2)}) copy-start(s32[4,8]{1,0:T(4,128)} %param.30) | copy-start | bytes 388
  0.7 14.8 %copy-start.12 = (bf16[1024,32]{0,1:T(8,128)(2,1)S(1)}, bf16[1024,32]{0,1:T(8,128)(2,1)}, u32[]{:S(2)}) copy-start(bf16[1024,32]{0,1:T(8,128)(2,1)} %param.23) | copy-start | bytes 196612
  0.7 27.3 %copy-start.14 = (f32[1024]{0:T(1024)S(1)}, f32[1024]{0:T(1024)}, u32[]{:S(2)}) copy-start(f32[1024]{0:T(1024)} %param.24) | copy-start | bytes 12292
  7.7 109.4 %all-to-all-start = ((bf16[4,128,1024]{2,1,0:T(8,128)(2,1)}), bf16[4,128,1024]{2,1,0:T(8,128)(2,1)}, u32[]{:S(2)}, u32[]{:S(2)}) async-start(bf16[4,128,1024]{2,1,0:T(8,128)(2,1)} %gather_fusion), calls=%async_computation | async-start | bytes 2097152 | tf_op jit(solution)/shard_map/all_to_all | solution.py:41
  44.6 64.8 %copy-start.5 = (s32[4,8]{1,0:T(4,128)S(1)}, s32[4,8]{1,0:T(4,128)}, u32[]{:S(2)}) copy-start(s32[4,8]{1,0:T(4,128)} %param.31) | copy-start | bytes 388
  44.6 4.5 %copy-start.2 = (bf16[1024,8,128]{2,0,1:T(8,128)(2,1)S(1)}, bf16[1024,8,128]{2,0,1:T(8,128)(2,1)}, u32[]{:S(2)}) copy-start(bf16[1024,8,128]{2,0,1:T(8,128)(2,1)} %get-tuple-element.357) | copy-start | bytes 6291460 | tf_op jit(solution)/shard_map/while
  56.5 8.6 %copy-start.6 = (bf16[1,512,8,128]{3,2,1,0:T(8,128)(2,1)S(1)}, bf16[1,512,8,128]{3,2,1,0:T(8,128)(2,1)}, u32[]{:S(2)}) copy-start(bf16[1,512,8,128]{3,2,1,0:T(8,128)(2,1)} %get-tuple-element.330) | copy-start | bytes 3145732 | tf_op jit(solution)/shard_map/while
  56.5 8.6 %copy-start.7 = (f32[8,1024,128]{2,1,0:T(8,128)S(1)}, f32[8,1024,128]{2,1,0:T(8,128)}, u32[]{:S(2)}) copy-start(f32[8,1024,128]{2,1,0:T(8,128)} %get-tuple-element.344) | copy-start | bytes 12582916 | tf_op jit(solution)/shard_map/while
  74.9 1.9 copy-start.8
  76.9 4.5 %copy-start.2 = (bf16[1024,8,128]{2,0,1:T(8,128)(2,1)S(1)}, bf16[1024,8,128]{2,0,1:T(8,128)(2,1)}, u32[]{:S(2)}) copy-start(bf16[1024,8,128]{2,0,1:T(8,128)(2,1)} %get-tuple-element.357) | copy-start | bytes 6291460 | tf_op jit(solution)/shard_map/while
  88.8 8.6 %copy-start.6 = (bf16[1,512,8,128]{3,2,1,0:T(8,128)(2,1)S(1)}, bf16[1,512,8,128]{3,2,1,0:T(8,128)(2,1)}, u32[]{:S(2)}) copy-start(bf16[1,512,8,128]{3,2,1,0:T(8,128)(2,1)} %get-tuple-element.330) | copy-start | bytes 3145732 | tf_op jit(solution)/shard_map/while
  88.8 8.6 %copy-start.7 = (f32[8,1024,128]{2,1,0:T(8,128)S(1)}, f32[8,1024,128]{2,1,0:T(8,128)}, u32[]{:S(2)}) copy-start(f32[8,1024,128]{2,1,0:T(8,128)} %get-tuple-element.344) | copy-start | bytes 12582916 | tf_op jit(solution)/shard_map/while
  107.2 1.9 copy-start.8
  117.1 174.4 %all-to-all-start.1 = ((bf16[4,2,2,128,1024]{4,3,2,1,0:T(8,128)(2,1)}), bf16[4,2,2,128,1024]{4,3,2,1,0:T(8,128)(2,1)}, u32[]{:S(2)}, u32[]{:S(2)}) async-start(bf16[4,2,2,128,1024]{4,3,2,1,0:T(8,128)(2,1)} %bitcast.159), calls=%async_computation.1 | async-start | bytes 8388608 | tf_op jit(solution)/shard_map/all_to_all | solution.py:113
  126.9 0.8 copy-start.16
  286.9 2.8 copy-start.11
  286.9 2.8 copy-start.13
  289.7 1.9 copy-start.3
  294.5 2.5 copy-start.9
  302.5 1.9 copy-start.10
  307.4 2.5 copy-start.9
  315.3 1.9 copy-start.10
  320.2 2.5 copy-start.9
  328.2 1.9 copy-start.10
  333.1 2.5 copy-start.9
  341.1 1.9 copy-start.10
  345.9 10.2 %copy-start.1 = (bf16[4,2,128,1024]{3,2,1,0:T(8,128)(2,1)S(1)}, bf16[4,2,128,1024]{3,2,1,0:T(8,128)(2,1)}, u32[]{:S(2)}) copy-start(bf16[4,2,128,1024]{3,2,1,0:T(8,128)(2,1)} %param.29) | copy-start | bytes 6291460
where the time goes:
time: 357 us; the launch traced here: 356 us
  matrix products  221 us (62%)
  local copies, waits for them, and re-layouts  62.5 us (18%)
  other arithmetic  44.7 us (13%)
  blocking collectives  12.6 us (4%)
  starting transfers between devices  11.3 us (3%)
    slice x1, matrix products, per_device(): mixed_sum = causal_filter(extended, kernel)[:, offset:offset + new_rows]  159 us
    dot_general x6, matrix products, fold_keys(): jnp.einsum('hqk,khd->hqd', weight.astype(jnp.bfloat16), value_rows, prefe...  41.3 us
    reduce_sum x6, other arithmetic, fold_keys(): running_sum = running_sum * shrink + jnp.sum(weight, axis=2)  26.4 us
    dot_general x6, matrix products, fold_keys(): jnp.einsum('qhd,khd->hqk', queries, key_rows, preferred_element_type=jnp....  20.4 us
    unnamed x26, local copies, waits for them, and re-layouts  15 us
    all_gather x1, blocking collectives, per_device(): filter_full = lax.all_gather(filter_taps, 'req', axis=1, tiled=True)  12.6 us
    while x46, local copies, waits for them, and re-layouts  12.5 us
  transfers between devices with their start and end apart: 2, of which 0 were waited for; matrix products, arithmetic and copies ran while one was open for 71% of the time, Pallas kernels for 0%

commit v1 on v0

--- a/solution.py
+++ b/solution.py
@@ -6,6 +6,18 @@
 
 HD = 128
 CAP = 2
+
+
+def gather_by_bits(shard, axis, dim):
+    ways, here = (lax.axis_size(axis), lax.axis_index(axis))
+    grown, reach = (shard, 1)
+    while reach < ways:
+        theirs = lax.ppermute(grown, axis, [(d, d ^ reach) for d in range(ways)])
+        mine_first = jnp.concatenate([grown, theirs], axis=dim)
+        theirs_first = jnp.concatenate([theirs, grown], axis=dim)
+        grown = jnp.where(here & reach == 0, mine_first, theirs_first)
+        reach = 2 * reach
+    return grown
 
 
 def causal_filter(extended, kernel):
@@ -64,7 +76,7 @@
     block_rows = hy_cache.shape[1]
     positions = jnp.arange(new_rows, dtype=jnp.int32)
     row_live = positions < new_length[0]
-    filter_full = lax.all_gather(filter_taps, "req", axis=1, tiled=True)
+    filter_full = gather_by_bits(filter_taps, "req", 1)
     filter_len = filter_full.shape[1]
     lag_steps = jnp.arange(filter_len, dtype=jnp.float32)
     kernel = (

time: 357 us -> 346 us (0.969)
  blocking collectives: 12.6 us -> 0 us
    all_gather x1 -> x0, blocking collectives: 12.6 us -> none  [per_device(): filter_full = lax.all_gather(filter_taps, 'req', axis=1, tiled=True)]
  transfers between devices with their start and end apart: 2 -> 4, of which waited for: 0 -> 0; matrix products, arithmetic and copies ran while one was open for 71% -> 76% of each run, Pallas kernels for 0% -> 0%
where the time goes in v1:
time: 346 us; the launch traced here: 345 us
  matrix products  221 us (64%)
  local copies, waits for them, and re-layouts  62.2 us (18%)
  other arithmetic  45.3 us (13%)
  starting transfers between devices  12.3 us (4%)
  between operations  3.48 us (1%)
    slice x1, matrix products, per_device(): mixed_sum = causal_filter(extended, kernel)[:, offset:offset + new_rows]  159 us
    dot_general x6, matrix products, fold_keys(): jnp.einsum('hqk,khd->hqd', weight.astype(jnp.bfloat16), value_rows, prefe...  41.3 us
    reduce_sum x6, other arithmetic, fold_keys(): running_sum = running_sum * shrink + jnp.sum(weight, axis=2)  26.4 us
    dot_general x6, matrix products, fold_keys(): jnp.einsum('qhd,khd->hqk', queries, key_rows, preferred_element_type=jnp....  20.4 us
    unnamed x26, local copies, waits for them, and re-layouts  15 us
    while x46, local copies, waits for them, and re-layouts  12.4 us
  transfers between devices with their start and end apart: 4, of which 0 were waited for; matrix products, arithmetic and copies ran while one was open for 76% of the time, Pallas kernels for 0%

profile of v1, /device:TPU:19, one launch (start us, length us, event | category | flops | bytes accessed | tf_op | source)
XLA Modules:
  0.0 344.8 jit_solution(2413005360602296712)
XLA Ops:
  2.1 1.3 gather_fusion.3
  3.4 1.3 gather_fusion.2
  5.4 2.8 gather_fusion
  8.3 4.5 %all-to-all-start = ((bf16[4,128,1024]{2,1,0:T(8,128)(2,1)}), bf16[4,128,1024]{2,1,0:T(8,128)(2,1)}, u32[]{:S(2)}, u32[]{:S(2)}) async-start(bf16[4,128,1024]{2,1,0:T(8,128)(2,1)} %gather_fusion), calls=%async_computation | async-start | bytes 2097152 | tf_op jit(solution)/shard_map/all_to_all | solution.py:53
  13.5 3.5 %copy.75 = bf16[128,8,8,128]{3,2,1,0:T(8,128)(2,1)} copy(bf16[128,8,8,128]{3,1,2,0:T(8,128)(2,1)} %bitcast.163) | data formatting | bytes 4194304
  17.1 3.9 %copy.60 = bf16[1,1024,1024]{1,2,0:T(8,128)(2,1)} copy(bf16[1,1024,1024]{2,1,0:T(8,128)(2,1)} %param.26) | data formatting | bytes 4194304 | tf_op args[6]
  21.0 3.9 %copy.62 = bf16[1024,8,128]{2,0,1:T(8,128)(2,1)} copy(bf16[1024,8,128]{0,2,1:T(8,128)(2,1)} %bitcast.162) | data formatting | bytes 4194304
  24.9 3.5 %copy.76 = bf16[128,8,8,128]{3,2,1,0:T(8,128)(2,1)} copy(bf16[128,8,8,128]{3,1,2,0:T(8,128)(2,1)} %bitcast.164) | data formatting | bytes 4194304
  28.4 64.2 %while.30 = (s32[]{:T(128)}, f32[8,1024]{1,0:T(8,128)S(1)}, f32[8,1024]{1,0:T(8,128)S(1)}, f32[8,1024,128]{2,1,0:T(8,128)}, s32[2]{0:T(128)S(1)}, /*index=5*/bf1...) while((s32[]{:T(128)}, f32[8,1024]{1,0:T(8,128)S(1)}, ...), condition=%wide.region_3.5_spmd.clone, body=%wide.region_0.4_spmd.clone.sunk | while | flops 2205721088 | bytes 115872000 | solution.py:110
  30.0 2.7 constant_dynamic-slice_fusion.10
  32.8 7.5 %fusion.90 = (f32[8,1024]{1,0:T(8,128)S(1)}, f32[8,512,1024]{2,1,0:T(8,128)}) fusion(pred[1024,512]{0,1:T(8,128)(4,1)S(1)} %iota_compare_fusion.9, bf16[1024,8,128]{2,0,1:T(8,128)(2,1)S(1)} %copy-done.2, bf16[1,512,8,128]{3,2,1,0:T(8,128)(2,1)S(1)} %get-tuple-element.325), kind=kOutput, calls=%fused_computation.34.clone.1 | convolution fusion | flops 1086316544 | bytes 20480000 | tf_op jit(solution)/shard_map/while/body/eval_jaxpr/qhd,khd->hqk/dot_general | solution.py:38
  40.2 8.6 %fusion.91 = f32[8,1024]{1,0:T(8,128)S(1)} fusion(f32[8,512,1024]{2,1,0:T(8,128)} %get-tuple-element.327, f32[8,1024]{1,0:T(8,128)S(1)} %select_maximum_fusion.2, pred[1024,512]{0,1:T(8,128)(4,1)S(1)} %iota_compare_fusion.9), kind=kLoop, calls=%fused_computation.36.clone.1 | loop fusion | flops 20963328 | bytes 17367040 | tf_op jit(solution)/shard_map/while/body/eval_jaxpr/reduce_sum | solution.py:45
  48.9 9.7 %fusion.93 = f32[8,1024,128]{2,1,0:T(8,128)S(1)} fusion(f32[8,1024,128]{2,1,0:T(8,128)S(1)} %copy-done.8, f32[8,1024]{1,0:T(8,128)S(1)} %get-tuple-element.329, pred[]{:T(512)S(6)} %compare.29, f32[8,512,1024]{2,1,0:T(8,128)} %get-tuple-element.327, f32[8,1024]{1,0:T(8,128)S(1)} %select_maximum_fusion.2, ...), kind=kOutput, calls=%fused_computation.40.clone.1 | convolution fusion | flops 1097859072 | bytes 26804224 | tf_op jit(solution)/shard_map/while/body/eval_jaxpr/hqk,khd->hqd/dot_general | solution.py:46
  58.6 1.9 copy-done.9
  62.1 2.7 constant_dynamic-slice_fusion.10
  64.9 7.4 %fusion.90 = (f32[8,1024]{1,0:T(8,128)S(1)}, f32[8,512,1024]{2,1,0:T(8,128)}) fusion(pred[1024,512]{0,1:T(8,128)(4,1)S(1)} %iota_compare_fusion.9, bf16[1024,8,128]{2,0,1:T(8,128)(2,1)S(1)} %copy-done.2, bf16[1,512,8,128]{3,2,1,0:T(8,128)(2,1)S(1)} %get-tuple-element.325), kind=kOutput, calls=%fused_computation.34.clone.1 | convolution fusion | flops 1086316544 | bytes 20480000 | tf_op jit(solution)/shard_map/while/body/eval_jaxpr/qhd,khd->hqk/dot_general | solution.py:38
  72.3 8.6 %fusion.91 = f32[8,1024]{1,0:T(8,128)S(1)} fusion(f32[8,512,1024]{2,1,0:T(8,128)} %get-tuple-element.327, f32[8,1024]{1,0:T(8,128)S(1)} %select_maximum_fusion.2, pred[1024,512]{0,1:T(8,128)(4,1)S(1)} %iota_compare_fusion.9), kind=kLoop, calls=%fused_computation.36.clone.1 | loop fusion | flops 20963328 | bytes 17367040 | tf_op jit(solution)/shard_map/while/body/eval_jaxpr/reduce_sum | solution.py:45
  81.0 9.7 %fusion.93 = f32[8,1024,128]{2,1,0:T(8,128)S(1)} fusion(f32[8,1024,128]{2,1,0:T(8,128)S(1)} %copy-done.8, f32[8,1024]{1,0:T(8,128)S(1)} %get-tuple-element.329, pred[]{:T(512)S(6)} %compare.29, f32[8,512,1024]{2,1,0:T(8,128)} %get-tuple-element.327, f32[8,1024]{1,0:T(8,128)S(1)} %select_maximum_fusion.2, ...), kind=kOutput, calls=%fused_computation.40.clone.1 | convolution fusion | flops 1097859072 | bytes 26804224 | tf_op jit(solution)/shard_map/while/body/eval_jaxpr/hqk,khd->hqd/dot_general | solution.py:46
  90.7 1.9 copy-done.9
  93.7 4.5 %multiply_convert_fusion = bf16[1,1024,1024]{2,1,0:T(8,128)(2,1)} fusion(bf16[1,1024,1024]{2,1,0:T(8,128)(2,1)} %param.22, bf16[1,1024,1024]{2,1,0:T(8,128)(2,1)} %param.21), kind=kLoop, calls=%fused_computation.71 | loop fusion | flops 4194304 | bytes 6291456 | tf_op jit(solution)/shard_map/convert_element_type | solution.py:146
  102.0 2.8 gather_fusion.1
  105.3 6.9 %all-to-all-start.1 = ((bf16[4,2,2,128,1024]{4,3,2,1,0:T(8,128)(2,1)}), bf16[4,2,2,128,1024]{4,3,2,1,0:T(8,128)(2,1)}, u32[]{:S(2)}, u32[]{:S(2)}) async-start(bf16[4,2,2,128,1024]{4,3,2,1,0:T(8,128)(2,1)} %bitcast.159), calls=%async_computation.1 | async-start | bytes 8388608 | tf_op jit(solution)/shard_map/all_to_all | solution.py:125
  113.8 1.3 copy.57
  116.4 159.2 %broadcast_select_fusion = f32[8,144,1024]{2,0,1:T(8,128)S(1)} fusion(pred[8,144]{0,1:T(8,128)(4,1)S(1)} %copy-done.16, bf16[128,1,1024]{2,0,1:T(8,128)(2,1)S(1)} %bitcast.165, bf16[8,271,1024]{2,0,1:T(8,128)(2,1)S(1)} %fusion.70), kind=kOutput, calls=%fused_computation.73 | convolution fusion | flops 303169536 | bytes 9421952 | tf_op jit(solution)/shard_map/slice | solution.py:149
  275.7 2.7 copy.59
  278.4 1.8 fusion.47
  280.3 51.4 %while.29 = (s32[]{:T(128)}, f32[8,1024]{1,0:T(8,128)S(1)}, f32[8,1024]{1,0:T(8,128)S(1)}, f32[8,1024,128]{2,1,0:T(8,128)}, pred[4,2]{1,0:T(4,128)(4,1)S(1)}, /*...) while((s32[]{:T(128)}, f32[8,1024]{1,0:T(8,128)S(1)}, ...), condition=%wide.region_10.12_spmd, body=%wide.region_7.11_spmd.sunk | while | flops 1103118336 | bytes 77071520 | solution.py:144
  280.4 1.3 copy_bitcast_fusion.7
  281.8 1.4 bitcast_reduce_fusion.2
  283.2 2.3 fusion.87
  285.7 5.5 %multiply_add_fusion.5 = f32[8,1024,128]{2,1,0:T(8,128)S(1)} fusion(f32[8,1024,128]{2,1,0:T(8,128)S(1)} %copy-done.10, f32[8,1024]{1,0:T(8,128)S(1)} %get-tuple-element.315, f32[8,256,1024]{2,1,0:T(8,128)S(1)} %get-tuple-element.313, f32[8,1024]{1,0:T(8,128)S(1)} %max.10, pred[256]{0:T(512)(128)(4,1)S(1)} %broadcast_bitcast_fusion.2, ...), kind=kOutput, calls=%fused_computation.13.clone.1 | convolution fusion | flops 549453824 | bytes 17367296 | tf_op jit(solution)/shard_map/while/body/eval_jaxpr/hqk,khd->hqd/dot_general | solution.py:46
  291.2 1.9 copy-done.11
  294.7 1.4 bitcast_reduce_fusion.2
  296.1 2.3 fusion.87
  298.6 5.5 %multiply_add_fusion.5 = f32[8,1024,128]{2,1,0:T(8,128)S(1)} fusion(f32[8,1024,128]{2,1,0:T(8,128)S(1)} %copy-done.10, f32[8,1024]{1,0:T(8,128)S(1)} %get-tuple-element.315, f32[8,256,1024]{2,1,0:T(8,128)S(1)} %get-tuple-element.313, f32[8,1024]{1,0:T(8,128)S(1)} %max.10, pred[256]{0:T(512)(128)(4,1)S(1)} %broadcast_bitcast_fusion.2, ...), kind=kOutput, calls=%fused_computation.13.clone.1 | convolution fusion | flops 549453824 | bytes 17367296 | tf_op jit(solution)/shard_map/while/body/eval_jaxpr/hqk,khd->hqd/dot_general | solution.py:46
  304.1 1.9 copy-done.11
  307.5 1.4 bitcast_reduce_fusion.2
  309.0 2.3 fusion.87
  311.4 5.5 %multiply_add_fusion.5 = f32[8,1024,128]{2,1,0:T(8,128)S(1)} fusion(f32[8,1024,128]{2,1,0:T(8,128)S(1)} %copy-done.10, f32[8,1024]{1,0:T(8,128)S(1)} %get-tuple-element.315, f32[8,256,1024]{2,1,0:T(8,128)S(1)} %get-tuple-element.313, f32[8,1024]{1,0:T(8,128)S(1)} %max.10, pred[256]{0:T(512)(128)(4,1)S(1)} %broadcast_bitcast_fusion.2, ...), kind=kOutput, calls=%fused_computation.13.clone.1 | convolution fusion | flops 549453824 | bytes 17367296 | tf_op jit(solution)/shard_map/while/body/eval_jaxpr/hqk,khd->hqd/dot_general | solution.py:46
  316.9 1.9 copy-done.11
  320.4 1.4 bitcast_reduce_fusion.2
  321.8 2.3 fusion.87
  324.3 5.5 %multiply_add_fusion.5 = f32[8,1024,128]{2,1,0:T(8,128)S(1)} fusion(f32[8,1024,128]{2,1,0:T(8,128)S(1)} %copy-done.10, f32[8,1024]{1,0:T(8,128)S(1)} %get-tuple-element.315, f32[8,256,1024]{2,1,0:T(8,128)S(1)} %get-tuple-element.313, f32[8,1024]{1,0:T(8,128)S(1)} %max.10, pred[256]{0:T(512)(128)(4,1)S(1)} %broadcast_bitcast_fusion.2, ...), kind=kOutput, calls=%fused_computation.13.clone.1 | convolution fusion | flops 549453824 | bytes 17367296 | tf_op jit(solution)/shard_map/while/body/eval_jaxpr/hqk,khd->hqd/dot_general | solution.py:46
  329.8 1.9 copy-done.11
  331.7 2.9 divide_bitcast_fusion
  334.6 2.7 copy.67
  337.3 4.2 %reshape.131 = bf16[1,1024,1024]{2,1,0:T(8,128)(2,1)} reshape(bf16[1024,8,128]{2,1,0:T(8,128)(2,1)} %copy.67) | data formatting | bytes 4194304 | tf_op jit(solution)/shard_map/reshape | solution.py:155
  341.4 3.3 select_convert_fusion
  (134 shorter events, 17.0 us)
Async XLA Ops:
  0.6 101.4 %copy-start = (bf16[4,2,128,1024]{3,2,1,0:T(8,128)(2,1)S(1)}, bf16[4,2,128,1024]{3,2,1,0:T(8,128)(2,1)}, u32[]{:S(2)}) copy-start(bf16[4,2,128,1024]{3,2,1,0:T(8,128)(2,1)} %param.29) | copy-start | bytes 6291460
  0.6 12.2 %copy-start.15 = (s32[4]{0:T(128)S(1)}, s32[4]{0:T(128)}, u32[]{:S(2)}) copy-start(s32[4]{0:T(128)} %param.32) | copy-start | bytes 52
  0.7 12.2 %copy-start.4 = (s32[4,8]{1,0:T(4,128)S(1)}, s32[4,8]{1,0:T(4,128)}, u32[]{:S(2)}) copy-start(s32[4,8]{1,0:T(4,128)} %param.30) | copy-start | bytes 388
  0.7 97.9 %collective-permute-start = (bf16[1024,32]{0,1:T(8,128)(2,1)}, bf16[1024,32]{0,1:T(8,128)(2,1)S(1)}, u32[]{:S(2)}, u32[]{:S(2)}) collective-permute-start(bf16[1024,32]{0,1:T(8,128)(2,1)} %param.23), channel_id=1, source_target_pairs={{0,4},{4,0},{8,12},{12,8},{1,5},{5,1},{9,13},{13,9},{2,6},{6,2},{1... | collective-permute-start | bytes 196616 | tf_op jit(solution)/shard_map/ppermute | solution.py:15
  8.3 97.0 %all-to-all-start = ((bf16[4,128,1024]{2,1,0:T(8,128)(2,1)}), bf16[4,128,1024]{2,1,0:T(8,128)(2,1)}, u32[]{:S(2)}, u32[]{:S(2)}) async-start(bf16[4,128,1024]{2,1,0:T(8,128)(2,1)} %gather_fusion), calls=%async_computation | async-start | bytes 2097152 | tf_op jit(solution)/shard_map/all_to_all | solution.py:53
  28.4 65.1 %copy-start.5 = (s32[4,8]{1,0:T(4,128)S(1)}, s32[4,8]{1,0:T(4,128)}, u32[]{:S(2)}) copy-start(s32[4,8]{1,0:T(4,128)} %param.31) | copy-start | bytes 388
  28.4 4.3 %copy-start.2 = (bf16[1024,8,128]{2,0,1:T(8,128)(2,1)S(1)}, bf16[1024,8,128]{2,0,1:T(8,128)(2,1)}, u32[]{:S(2)}) copy-start(bf16[1024,8,128]{2,0,1:T(8,128)(2,1)} %get-tuple-element.357) | copy-start | bytes 6291460 | tf_op jit(solution)/shard_map/while
  40.2 8.6 %copy-start.6 = (bf16[1,512,8,128]{3,2,1,0:T(8,128)(2,1)S(1)}, bf16[1,512,8,128]{3,2,1,0:T(8,128)(2,1)}, u32[]{:S(2)}) copy-start(bf16[1,512,8,128]{3,2,1,0:T(8,128)(2,1)} %get-tuple-element.330) | copy-start | bytes 3145732 | tf_op jit(solution)/shard_map/while
  40.2 8.6 %copy-start.8 = (f32[8,1024,128]{2,1,0:T(8,128)S(1)}, f32[8,1024,128]{2,1,0:T(8,128)}, u32[]{:S(2)}) copy-start(f32[8,1024,128]{2,1,0:T(8,128)} %get-tuple-element.344) | copy-start | bytes 12582916 | tf_op jit(solution)/shard_map/while
  58.6 1.9 copy-start.9
  60.6 4.3 %copy-start.2 = (bf16[1024,8,128]{2,0,1:T(8,128)(2,1)S(1)}, bf16[1024,8,128]{2,0,1:T(8,128)(2,1)}, u32[]{:S(2)}) copy-start(bf16[1024,8,128]{2,0,1:T(8,128)(2,1)} %get-tuple-element.357) | copy-start | bytes 6291460 | tf_op jit(solution)/shard_map/while
  72.3 8.6 %copy-start.6 = (bf16[1,512,8,128]{3,2,1,0:T(8,128)(2,1)S(1)}, bf16[1,512,8,128]{3,2,1,0:T(8,128)(2,1)}, u32[]{:S(2)}) copy-start(bf16[1,512,8,128]{3,2,1,0:T(8,128)(2,1)} %get-tuple-element.330) | copy-start | bytes 3145732 | tf_op jit(solution)/shard_map/while
  72.3 8.6 %copy-start.8 = (f32[8,1024,128]{2,1,0:T(8,128)S(1)}, f32[8,1024,128]{2,1,0:T(8,128)}, u32[]{:S(2)}) copy-start(f32[8,1024,128]{2,1,0:T(8,128)} %get-tuple-element.344) | copy-start | bytes 12582916 | tf_op jit(solution)/shard_map/while
  90.7 1.9 copy-start.9
  92.7 5.9 %copy-start.13 = (bf16[1024,32]{0,1:T(8,128)(2,1)S(1)}, bf16[1024,32]{0,1:T(8,128)(2,1)}, u32[]{:S(2)}) copy-start(bf16[1024,32]{0,1:T(8,128)(2,1)} %param.23) | copy-start | bytes 196612
  92.7 8.0 %copy-start.14 = (f32[1024]{0:T(1024)S(1)}, f32[1024]{0:T(1024)}, u32[]{:S(2)}) copy-start(f32[1024]{0:T(1024)} %param.24) | copy-start | bytes 12292
  98.6 6.2 %collective-permute-start.1 = (bf16[1024,64]{0,1:T(8,128)(2,1)S(1)}, bf16[1024,64]{0,1:T(8,128)(2,1)S(1)}, u32[]{:S(2)}, u32[]{:S(2)}) collective-permute-start(bf16[1024,64]{0,1:T(8,128)(2,1)S(1)} %maximum_select_fusion.1), channel_id=1, source_target_pairs={{0,8},{4,12},{8,0},{12,4},{1,9},{5,13},{9,1},{13,5},{2,10},{6,14},... | collective-permute-start | bytes 393224 | tf_op jit(solution)/shard_map/ppermute | solution.py:15
  105.3 7.9 %copy-start.7 = (bf16[1,1024,1024]{2,1,0:T(8,128)(2,1)S(1)}, bf16[1,1024,1024]{2,1,0:T(8,128)(2,1)}, u32[]{:S(2)}) copy-start(bf16[1,1024,1024]{2,1,0:T(8,128)(2,1)} %multiply_convert_fusion) | copy-start | bytes 6291460
  105.3 175.0 %all-to-all-start.1 = ((bf16[4,2,2,128,1024]{4,3,2,1,0:T(8,128)(2,1)}), bf16[4,2,2,128,1024]{4,3,2,1,0:T(8,128)(2,1)}, u32[]{:S(2)}, u32[]{:S(2)}) async-start(bf16[4,2,2,128,1024]{4,3,2,1,0:T(8,128)(2,1)} %bitcast.159), calls=%async_computation.1 | async-start | bytes 8388608 | tf_op jit(solution)/shard_map/all_to_all | solution.py:125
  115.6 0.8 copy-start.16
  275.6 2.8 copy-start.12
  278.4 1.9 copy-start.3
  283.2 2.5 copy-start.10
  291.2 1.9 copy-start.11
  296.1 2.5 copy-start.10
  304.0 1.9 copy-start.11
  308.9 2.5 copy-start.10
  316.9 1.9 copy-start.11
  321.8 2.5 copy-start.10
  329.8 1.9 copy-start.11
  334.6 10.2 %copy-start.1 = (bf16[4,2,128,1024]{3,2,1,0:T(8,128)(2,1)S(1)}, bf16[4,2,128,1024]{3,2,1,0:T(8,128)(2,1)}, u32[]{:S(2)}) copy-start(bf16[4,2,128,1024]{3,2,1,0:T(8,128)(2,1)} %param.29) | copy-start | bytes 6291460
